TPU v7x, 32 devices: a whole 2x2x4 slice. The times are simulated.
32 devices in a mesh: member: 2 (over x), ty: 16 (over z, y, core).
Axes of the slice: x: 2, y: 2, z: 4, core: 2. Of those that a mesh axis runs over, the one named last changes fastest.
Arguments:
- fields: float32 [32, 768, 6, 768], P('member', 'ty'), parts along dimension 0, may hold values from -6 to 6
- damp_four: float32 [32], P('member'), parts along dimension 0, may hold values from 0.004 to 0.03
- damp_six: float32 [32], P('member'), parts along dimension 0, may hold values from 0.0008 to 0.006
- metric: float32 [4, 768, 6, 768], P(None, 'ty'), may hold values from 0.1 to 1.9
- seam_table: int32 [6, 4, 3], replicated, may hold values from 0 to 5
Outputs:
- damped: float32 [32, 768, 6, 768], P('member', 'ty'), parts along dimension 0
There are 2 independent parts, one for each index of `member`. A program takes and returns all parts, laid end to end along the dimension named above; an argument that names none is the same for every part. Nothing has to cross between parts.
Inputs may be any that keep to these rules, and one draw needn't show every extreme that they name: The table describes the surface of a cube with every face seen from outside: the joining is symmetric, no face is joined to itself, and r is 1 exactly when both edges are among (south, east) or both among (north, west).
All inputs are finite; a program needn't handle non-finite values.
Results may differ from a plain program's by a relative error of at most 0.00005.
Values sent between devices are 32-bit elements; how exact they have to be, the bound alone decides.
A program may use at most 128 MiB of HBM per device.

v0:
```python
import jax
import jax.numpy as jnp
from jax import lax
from jax.sharding import PartitionSpec as P


def with_halo(cells, sides, width):
    for axis, dim in sides:
        count = lax.axis_size(axis)
        ends = count - 1
        head = lax.slice_in_dim(cells, 0, width, axis=dim)
        tail = lax.slice_in_dim(cells, cells.shape[dim] - width, cells.shape[dim], axis=dim)
        cells = jnp.concatenate(
            [
                lax.ppermute(tail, axis, [(i, (i + 1) % count) for i in range(ends)]),
                cells,
                lax.ppermute(head, axis, [((i + 1) % count, i) for i in range(ends)]),
            ],
            axis=dim,
        )
    return cells


def strip_edges(source):
    east_cells = jnp.transpose(source[:, :, :, -1], (0, 2, 1))
    west_cells = jnp.transpose(source[:, :, :, 0], (0, 2, 1))
    return jnp.stack([east_cells, west_cells], axis=2)


def gather_edges(source):
    tile_index = lax.axis_index("ty")
    tile_count = lax.axis_size("ty")
    strip_rows = source.shape[1]
    row_width = source.shape[3]
    strip_cells = strip_edges(source)
    first_row = jnp.where(tile_index == 0, source[:, 0], 0.0)
    last_row = jnp.where(tile_index == tile_count - 1, source[:, -1], 0.0)
    blank = jnp.zeros(strip_cells.shape[:3] + (row_width,), jnp.float32)
    placed = lax.dynamic_update_slice_in_dim(blank, strip_cells, tile_index * strip_rows, 3)
    rim_cells = jnp.stack([first_row, placed[:, :, 0], last_row, placed[:, :, 1]], axis=2)
    edge_set = lax.psum(rim_cells, "ty")
    return edge_set


def seam_halo(edge_set, seam_table):
    levels = edge_set.shape[0]
    row_width = edge_set.shape[3]
    flattened = edge_set.reshape(levels, 24, row_width)
    picked = (seam_table[:, :, 0] * 4 + seam_table[:, :, 1]).reshape(24)
    onehot = (picked[:, None] == jnp.arange(24, dtype=jnp.int32)[None, :]).astype(jnp.float32)
    neighbor = jnp.einsum("jk,lkc->ljc", onehot, flattened, precision=lax.Precision.HIGHEST)
    neighbor = neighbor.reshape(levels, 6, 4, row_width)
    flipped = (seam_table[:, :, 2] == 1)[None, :, :, None]
    return jnp.where(flipped, neighbor[..., ::-1], neighbor)


def laplace(source, metric, seam_table):
    tile_index = lax.axis_index("ty")
    tile_count = lax.axis_size("ty")
    strip_rows = source.shape[1]
    padded = with_halo(source, (("ty", 1),), 1)
    halo_cells = seam_halo(gather_edges(source), seam_table)
    south_row = jnp.where(tile_index == 0, halo_cells[:, :, 0], padded[:, 0])
    north_row = jnp.where(tile_index == tile_count - 1, halo_cells[:, :, 2], padded[:, -1])
    row_start = tile_index * strip_rows
    west_cells = jnp.transpose(
        lax.dynamic_slice_in_dim(halo_cells[:, :, 3], row_start, strip_rows, 2), (0, 2, 1)
    )[..., None]
    east_cells = jnp.transpose(
        lax.dynamic_slice_in_dim(halo_cells[:, :, 1], row_start, strip_rows, 2), (0, 2, 1)
    )[..., None]
    padded_x = jnp.concatenate([west_cells, source, east_cells], axis=3)
    padded_y = jnp.concatenate([south_row[:, None], source, north_row[:, None]], axis=1)
    return (
        metric[0] * (padded_x[..., :-2] - source)
        + metric[1] * (padded_x[..., 2:] - source)
        + metric[2] * (padded_y[:, :-2] - source)
        + metric[3] * (padded_y[:, 2:] - source)
    )


def per_device(fields, damp_four, damp_six, metric, seam_table):
    second = laplace(fields, metric, seam_table)
    fourth = laplace(second, metric, seam_table)
    sixth = laplace(fourth, metric, seam_table)
    return fields - damp_four[:, None, None, None] * fourth + damp_six[:, None, None, None] * sixth


def solution(mesh):
    placed = (
        P("member", "ty", None, None),
        P("member"),
        P("member"),
        P(None, "ty", None, None),
        P(),
    )
    return jax.shard_map(
        per_device,
        mesh=mesh,
        in_specs=placed,
        out_specs=P("member", "ty", None, None),
        check_vma=False,
    )
```

profile of v0, /device:TPU:0, one launch (start us, length us, event | category | flops | bytes accessed | tf_op | source)
XLA Modules:
  0.0 596.8 jit_solution(6882728278029485408)
XLA Ops:
  6.5 4.6 fusion.54
  11.1 18.5 %copy.89 = f32[16,48,6,768]{3,0,2,1:T(8,128)} copy(f32[16,48,6,768]{3,1,2,0:T(8,128)} %param.5) | data formatting | bytes 28311552 | tf_op args[0]
  38.1 4.7 collective-permute-start
  49.8 88.0 %all-reduce.4.cloned.1.call-done = f32[16,24,768]{2,1,0:T(8,128)} async-done(((f32[16,24,768]{2,1,0:T(8,128)}), f32[16,24,768]{2,1,0:T(8,128)}) %all-reduce.4.cloned.1.call-update) | async-done | bytes 1179664 | tf_op jit(solution)/shard_map/psum | solution.py:41
  141.1 4.7 rev.9
  150.1 3.9 copy.68
  155.7 4.0 copy.73
  161.7 33.4 %fusion.26 = f32[16,48,6,768]{3,0,2,1:T(8,128)} fusion(f32[16,48,6,768]{3,0,2,1:T(8,128)} %copy.89, f32[16,1,6,768]{3,0,2,1:T(8,128)} %get-tuple-element.38, f32[16,1,6,768]{3,0,2,1:T(8,128)} %get-tuple-element.37, f32[16,48,6,1]{3,0,2,1:T(8,128)} %copy.73, f32[16,48,6,1]{3,0,2,1:T(8,128)} %copy.68, f32[48,6,768]{2,1,0:T(8,128)} %copy.79, ...), kind=kLoop, calls=%fused_computation.35 | loop fusion | flops 53084160 | bytes 32477184 | tf_op jit(solution)/shard_map/add | solution.py:75
  195.1 5.3 fusion.52
  202.5 3.4 copy.104
  205.9 3.4 copy.83
  220.1 3.2 collective-permute-start.2
  224.6 91.8 %all-reduce.6.cloned.1.call-done = f32[16,24,768]{2,1,0:T(8,128)} async-done(((f32[16,24,768]{2,1,0:T(8,128)}), f32[16,24,768]{2,1,0:T(8,128)}) %all-reduce.6.cloned.1.call-update) | async-done | bytes 1179664 | tf_op jit(solution)/shard_map/psum | solution.py:41
  316.4 3.0 convolution_bitcast_fusion.1
  319.3 10.9 %reshape.133 = f32[16,6,4,768]{3,2,1,0:T(4,128)} reshape(f32[16,24,768]{2,1,0:T(8,128)} %convolution_bitcast_fusion.1) | data formatting | bytes 2359296 | tf_op jit(solution)/shard_map/reshape | solution.py:52
  330.3 2.7 copy.85
  332.9 4.7 rev.10
  342.1 3.9 copy.87
  347.7 4.0 copy.88
  353.7 34.7 %fusion.15 = f32[16,48,6,768]{3,0,2,1:T(8,128)} fusion(f32[16,48,6,768]{3,0,2,1:T(8,128)} %fusion.26, f32[16,1,6,768]{3,0,2,1:T(8,128)} %get-tuple-element.34, f32[16,1,6,768]{3,0,2,1:T(8,128)} %get-tuple-element.33, f32[16,48,6,1]{3,0,2,1:T(8,128)} %copy.88, f32[16,48,6,1]{3,0,2,1:T(8,128)} %copy.87, f32[48,6,768]{2,1,0:T(8,128)} %copy.79, ...), kind=kLoop, calls=%fused_computation.20 | loop fusion | flops 53084160 | bytes 32477184 | tf_op jit(solution)/shard_map/add | solution.py:75
  388.4 5.3 fusion.50
  395.8 3.4 copy.90
  399.2 3.4 copy.91
  410.7 2.8 reshape.134
  413.6 3.2 collective-permute-start.4
  418.1 91.7 %all-reduce.8.cloned.1.call-done = f32[16,24,768]{2,1,0:T(8,128)} async-done(((f32[16,24,768]{2,1,0:T(8,128)}), f32[16,24,768]{2,1,0:T(8,128)}) %all-reduce.8.cloned.1.call-update) | async-done | bytes 1179664 | tf_op jit(solution)/shard_map/psum | solution.py:41
  509.8 3.0 convolution_bitcast_fusion
  518.0 4.7 rev.11
  526.5 3.9 copy.97
  530.5 4.0 copy.98
  536.0 35.3 %fusion.4 = f32[16,48,6,768]{3,0,2,1:T(8,128)} fusion(f32[16,48,6,768]{3,0,2,1:T(8,128)} %fusion.15, f32[16,1,6,768]{3,0,2,1:T(8,128)S(1)} %get-tuple-element.30, f32[16,1,6,768]{3,0,2,1:T(8,128)S(1)} %get-tuple-element.29, f32[16,48,6,1]{3,0,2,1:T(8,128)} %copy.98, f32[16,48,6,1]{3,0,2,1:T(8,128)} %copy.97, f32[16]{0:T(128)S(1)} %copy-done.5, ...), kind=kLoop, calls=%fused_computation.5 | loop fusion | flops 67239936 | bytes 46633088 | tf_op jit(solution)/shard_map/add | solution.py:86
  571.3 18.5 %copy.99 = f32[16,48,6,768]{3,1,2,0:T(8,128)} copy(f32[16,48,6,768]{3,0,2,1:T(8,128)} %fusion.4) | data formatting | bytes 28311552 | tf_op jit(solution)/shard_map/add | solution.py:86
  (83 shorter events, 70.8 us)
Async XLA Ops:
  6.5 131.3 %all-reduce.4.cloned.1.call-start = ((), (), s32[]{:S(2)}) async-start(), calls=%async_computation | async-start | bytes 2359296 | tf_op jit(solution)/shard_map/psum | solution.py:41
  36.6 7.5 %copy-start.4 = (s32[6,4,3]{0,1,2:T(4,128)S(1)}, s32[6,4,3]{0,1,2:T(4,128)}, u32[]{:S(2)}) copy-start(s32[6,4,3]{0,1,2:T(4,128)} %param.9) | copy-start | bytes 868
  38.0 278.3 %all-reduce.6.cloned.1.call-start = ((), (), s32[]{:S(2)}) async-start(), calls=%async_computation.1 | async-start | bytes 2359296 | tf_op jit(solution)/shard_map/psum | solution.py:41
  38.1 121.6 %collective-permute-start = (f32[16,1,6,768]{3,0,2,1:T(8,128)}, f32[16,1,6,768]{3,0,2,1:T(8,128)}, u32[]{:S(2)}, u32[]{:S(2)}) collective-permute-start(f32[16,1,6,768]{3,0,2,1:T(8,128)} %get-tuple-element.17), channel_id=1, source_target_pairs={{0,1},{1,2},{2,3},{3,4},{4,5},{5,6},{6,7},{7,8},{8,9},{9,10},{10,1... | collective-permute-start | bytes 884744 | tf_op jit(solution)/shard_map/ppermute | solution.py:15
  42.8 116.8 %collective-permute-start.1 = (f32[16,1,6,768]{3,0,2,1:T(8,128)}, f32[16,1,6,768]{3,0,2,1:T(8,128)}, u32[]{:S(2)}, u32[]{:S(2)}) collective-permute-start(f32[16,1,6,768]{3,0,2,1:T(8,128)} %get-tuple-element.19), channel_id=1, source_target_pairs={{1,0},{2,1},{3,2},{4,3},{5,4},{6,5},{7,6},{8,7},{9,8},{10,9},{11,1... | collective-permute-start | bytes 884744 | tf_op jit(solution)/shard_map/ppermute | solution.py:17
  147.7 1.0 copy-start.2
  220.0 289.8 %all-reduce.8.cloned.1.call-start = ((), (), s32[]{:S(2)}) async-start(), calls=%async_computation.2 | async-start | bytes 2359296 | tf_op jit(solution)/shard_map/psum | solution.py:41
  220.1 131.6 %collective-permute-start.2 = (f32[16,1,6,768]{3,0,2,1:T(8,128)}, f32[16,1,6,768]{3,0,2,1:T(8,128)}, u32[]{:S(2)}, u32[]{:S(2)}) collective-permute-start(f32[16,1,6,768]{3,0,2,1:T(8,128)} %get-tuple-element.11), channel_id=1, source_target_pairs={{0,1},{1,2},{2,3},{3,4},{4,5},{5,6},{6,7},{7,8},{8,9},{9,10},{10,1... | collective-permute-start | bytes 884744 | tf_op jit(solution)/shard_map/ppermute | solution.py:15
  223.3 128.3 %collective-permute-start.3 = (f32[16,1,6,768]{3,0,2,1:T(8,128)}, f32[16,1,6,768]{3,0,2,1:T(8,128)}, u32[]{:S(2)}, u32[]{:S(2)}) collective-permute-start(f32[16,1,6,768]{3,0,2,1:T(8,128)} %get-tuple-element.14), channel_id=1, source_target_pairs={{1,0},{2,1},{3,2},{4,3},{5,4},{6,5},{7,6},{8,7},{9,8},{10,9},{11,1... | collective-permute-start | bytes 884744 | tf_op jit(solution)/shard_map/ppermute | solution.py:17
  339.7 1.0 copy-start.3
  413.6 120.9 %collective-permute-start.4 = (f32[16,1,6,768]{3,0,2,1:T(8,128)}, f32[16,1,6,768]{3,0,2,1:T(8,128)}, u32[]{:S(2)}, u32[]{:S(2)}) collective-permute-start(f32[16,1,6,768]{3,0,2,1:T(8,128)} %get-tuple-element.5), channel_id=1, source_target_pairs={{0,1},{1,2},{2,3},{3,4},{4,5},{5,6},{6,7},{7,8},{8,9},{9,10},{10,1... | collective-permute-start | bytes 884744 | tf_op jit(solution)/shard_map/ppermute | solution.py:15
  416.8 117.7 %collective-permute-start.5 = (f32[16,1,6,768]{3,0,2,1:T(8,128)}, f32[16,1,6,768]{3,0,2,1:T(8,128)}, u32[]{:S(2)}, u32[]{:S(2)}) collective-permute-start(f32[16,1,6,768]{3,0,2,1:T(8,128)} %get-tuple-element.8), channel_id=1, source_target_pairs={{1,0},{2,1},{3,2},{4,3},{5,4},{6,5},{7,6},{8,7},{9,8},{10,9},{11,1... | collective-permute-start | bytes 884744 | tf_op jit(solution)/shard_map/ppermute | solution.py:17
  524.7 1.0 copy-start.1
  530.5 5.4 copy-start.5
  530.5 5.4 copy-start.6
  534.5 1.5 copy-start
Sparse Core Ops, SparseCore 0:
  38.2 99.5 all-reduce.3
  220.1 96.1 all-reduce.5
  413.7 96.0 all-reduce.7
where the time goes:
time: 606 us; the launch traced here: 597 us
  waiting for transfers between devices  271 us (45%)
  local copies, waits for them, and re-layouts  162 us (27%)
  other arithmetic  126 us (21%)
  starting transfers between devices  15.1 us (2%)
  between operations  13.8 us (2%)
  matrix products  7.85 us (1%)
    psum x3, waiting for transfers between devices, gather_edges(): edge_set = lax.psum(rim_cells, 'ty')  271 us
    add x2, other arithmetic, laplace(): metric[0] * (padded_x[..., :-2] - source)  68.1 us
    add x1, other arithmetic, per_device(): fields - damp_four[:, None, None, None] * fourth  35.3 us
    unnamed x19, local copies, waits for them, and re-layouts  28.6 us
    reshape x5, local copies, waits for them, and re-layouts, seam_halo(): neighbor = neighbor.reshape(levels, 6, 4, row_width)  20.2 us
    slice x4, local copies, waits for them, and re-layouts, strip_edges(): east_cells = jnp.transpose(source[:, :, :, -1], (0, 2, 1))  18.6 us
    add x1, local copies, waits for them, and re-layouts, per_device(): fields - damp_four[:, None, None, None] * fourth  18.5 us
    broadcast_in_dim x6, local copies, waits for them, and re-layouts, laplace(): jnp.transpose(lax.dynamic_slice_in_dim(halo_cells[:, :, 1], row_start, st...  15.9 us
  transfers between devices with their start and end apart: 9, of which 3 were waited for; matrix products, arithmetic and copies ran while one was open for 14% of the time, Pallas kernels for 0%

commit v1 on v0

v1 whole, which is shorter than its diff:
```python
import functools

import jax
import jax.numpy as jnp
from jax import lax
from jax.experimental import pallas as pl
from jax.experimental.pallas import tpu as pltpu
from jax.sharding import PartitionSpec as P

LANES = 128


def exchange(south, north, west, east, seam_table):
    index = lax.axis_index("ty")
    count = lax.axis_size("ty")
    levels, faces, width = south.shape
    rows = west.shape[2]
    below = lax.ppermute(north, "ty", [(i, i + 1) for i in range(count - 1)])
    above = lax.ppermute(south, "ty", [(i + 1, i) for i in range(count - 1)])
    sides = jnp.stack([east, west], axis=2)
    blank = jnp.zeros((levels, faces, 2, width), jnp.float32)
    placed = lax.dynamic_update_slice_in_dim(blank, sides, index * rows, 3)
    first = jnp.where(index == 0, south, 0.0)
    last = jnp.where(index == count - 1, north, 0.0)
    rim = jnp.stack([first, placed[:, :, 0], last, placed[:, :, 1]], axis=2)
    edges = lax.psum(rim, "ty").reshape(levels, faces * 4, width)
    picked = (seam_table[:, :, 0] * 4 + seam_table[:, :, 1]).reshape(faces * 4)
    onehot = (picked[:, None] == jnp.arange(faces * 4, dtype=jnp.int32)[None, :]).astype(jnp.float32)
    near = jnp.einsum("jk,lkc->ljc", onehot, edges, precision=lax.Precision.HIGHEST)
    near = near.reshape(levels, faces, 4, width)
    flipped = (seam_table[:, :, 2] == 1)[None, :, :, None]
    halo = jnp.where(flipped, near[..., ::-1], near)
    start = index * rows
    return (
        jnp.where(index == 0, halo[:, :, 0], below),
        jnp.where(index == count - 1, halo[:, :, 2], above),
        lax.dynamic_slice_in_dim(halo[:, :, 3], start, rows, 2),
        lax.dynamic_slice_in_dim(halo[:, :, 1], start, rows, 2),
    )


def weigh(metric, cells, west, east, south, north):
    return (
        metric[0] * (west - cells)
        + metric[1] * (east - cells)
        + metric[2] * (south - cells)
        + metric[3] * (north - cells)
    )


def join(parts, axis):
    return jnp.concatenate(parts, axis=axis)


def frame_step(frame, halo, metric_rows, metric_cols):
    south, north, west, east = frame
    h_south, h_north, h_west, h_east = halo
    k = south.shape[2] - 1

    def along_x(lines, west_halo, east_halo):
        return (
            join([west_halo[..., None], lines[..., :-1]], 3),
            join([lines[..., 1:], east_halo[..., None]], 3),
        )

    c = south[:, :, :k]
    w, e = along_x(c, h_west[:, :, :k], h_east[:, :, :k])
    new_south = weigh(
        metric_rows[0][:, None, :, :k], c, w, e,
        join([h_south[:, :, None], south[:, :, : k - 1]], 2), south[:, :, 1:],
    )
    c = north[:, :, 1:]
    w, e = along_x(c, h_west[:, :, -k:], h_east[:, :, -k:])
    new_north = weigh(
        metric_rows[1][:, None, :, -k:], c, w, e,
        north[:, :, :-1], join([north[:, :, 2:], h_north[:, :, None]], 2),
    )
    c = west[:, :, :k]
    s, n = along_x(c, h_south[:, :, :k], h_north[:, :, :k])
    new_west = weigh(
        metric_cols[0][:, None, :, :k], c,
        join([h_west[:, :, None], west[:, :, : k - 1]], 2), west[:, :, 1:], s, n,
    )
    c = east[:, :, 1:]
    s, n = along_x(c, h_south[:, :, -k:], h_north[:, :, -k:])
    new_east = weigh(
        metric_cols[1][:, None, :, -k:], c,
        east[:, :, :-1], join([east[:, :, 2:], h_east[:, :, None]], 2), s, n,
    )
    return new_south, new_north, new_west, new_east


def halos_of(fields, metric, seam_table):
    def rim(array, k):
        return (
            array[:, :, :k],
            array[:, :, -k:],
            jnp.swapaxes(array[..., :k], 2, 3),
            jnp.swapaxes(array[..., -k:], 2, 3),
        )

    m_south, m_north, m_west, m_east = rim(metric, 2)
    frame = rim(fields, 3)
    rounds = []
    for step in range(3):
        south, north, west, east = frame
        halo = exchange(south[:, :, 0], north[:, :, -1], west[:, :, 0], east[:, :, -1], seam_table)
        rounds.append(halo)
        if step < 2:
            frame = frame_step(frame, halo, (m_south, m_north), (m_west, m_east))
    return rounds


def damp_kernel(four_ref, six_ref, v_ref, m_ref, hr_ref, hc_ref, o_ref, second_ref, fourth_ref):
    block, _, rows, width = v_ref.shape
    tiles = width // LANES
    levels = four_ref.shape[0]
    lane = lax.broadcasted_iota(jnp.int32, (rows, LANES), 1)
    row = lax.broadcasted_iota(jnp.int32, (rows, LANES), 0)
    aligned = rows % 8 == 0

    def at(t):
        return pl.ds(t * LANES, LANES)

    def one_level(j, carry):
        level = pl.program_id(1) * block + j

        def laplace(load, step, put):
            sides = hc_ref[0]
            before = pltpu.roll(sides, lax.rem(2 * LANES - 2 * step * levels - level, LANES), 1)
            beyond = pltpu.roll(
                sides, lax.rem(3 * LANES - 1 - (2 * step + 1) * levels - level, LANES), 1
            )
            right = [pltpu.roll(load(t), 1, 1) for t in range(tiles)]
            for t in range(tiles):
                c = load(t)
                left = pltpu.roll(c, LANES - 1, 1)
                after = pltpu.roll(load(t + 1), LANES - 1, 1) if t + 1 < tiles else beyond
                west = jnp.where(lane == 0, right[t - 1] if t > 0 else before, right[t])
                east = jnp.where(lane == LANES - 1, after, left)
                low = hr_ref[j, 0, 2 * step : 2 * step + 1, at(t)]
                high = hr_ref[j, 0, 2 * step + 1 : 2 * step + 2, at(t)]
                if aligned:
                    south = jnp.where(row == 0, low, pltpu.roll(c, 1, 0))
                    north = jnp.where(row == rows - 1, high, pltpu.roll(c, rows - 1, 0))
                else:
                    south = jnp.concatenate([low, c[:-1]], axis=0)
                    north = jnp.concatenate([c[1:], high], axis=0)
                put(
                    t,
                    m_ref[0, 0, :, at(t)] * (west - c)
                    + m_ref[1, 0, :, at(t)] * (east - c)
                    + m_ref[2, 0, :, at(t)] * (south - c)
                    + m_ref[3, 0, :, at(t)] * (north - c),
                )

        def put_second(t, x):
            second_ref[:, at(t)] = x

        def put_fourth(t, x):
            fourth_ref[:, at(t)] = x

        def put_out(t, x):
            o_ref[j, 0, :, at(t)] = (
                v_ref[j, 0, :, at(t)] - four_ref[level] * fourth_ref[:, at(t)] + six_ref[level] * x
            )

        laplace(lambda t: v_ref[j, 0, :, at(t)], 0, put_second)
        laplace(lambda t: second_ref[:, at(t)], 1, put_fourth)
        laplace(lambda t: fourth_ref[:, at(t)], 2, put_out)
        return carry

    lax.fori_loop(0, block, one_level, 0)


def damp(fields, damp_four, damp_six, metric, halo_rows, halo_cols):
    levels, faces, rows, width = fields.shape
    block = next(b for b in (4, 2, 1) if levels % b == 0)
    cells = fields.size
    return pl.pallas_call(
        damp_kernel,
        grid=(faces, levels // block),
        in_specs=[
            pl.BlockSpec(memory_space=pltpu.SMEM),
            pl.BlockSpec(memory_space=pltpu.SMEM),
            pl.BlockSpec((block, 1, rows, width), lambda f, l: (l, f, 0, 0)),
            pl.BlockSpec((4, 1, rows, width), lambda f, l: (0, f, 0, 0)),
            pl.BlockSpec((block, 1, 8, width), lambda f, l: (l, f, 0, 0)),
            pl.BlockSpec((1, rows, LANES), lambda f, l: (f, 0, 0)),
        ],
        out_specs=pl.BlockSpec((block, 1, rows, width), lambda f, l: (l, f, 0, 0)),
        out_shape=jax.ShapeDtypeStruct(fields.shape, jnp.float32),
        scratch_shapes=[
            pltpu.VMEM((rows, width), jnp.float32),
            pltpu.VMEM((rows, width), jnp.float32),
        ],
        cost_estimate=pl.CostEstimate(flops=40 * cells, bytes_accessed=10 * cells, transcendentals=0),
        name="damp",
    )(damp_four, damp_six, fields, metric, halo_rows, halo_cols)


def per_device(fields, damp_four, damp_six, metric, seam_table):
    fields = jnp.transpose(fields, (0, 2, 1, 3))
    metric = jnp.transpose(metric, (0, 2, 1, 3))
    levels, faces, rows, width = fields.shape
    rounds = halos_of(fields, metric, seam_table)
    halo_rows = jnp.stack([part for halo in rounds for part in halo[:2]], axis=2)
    halo_rows = jnp.pad(halo_rows, ((0, 0), (0, 0), (0, 2), (0, 0)))
    halo_cols = jnp.stack([part for halo in rounds for part in halo[2:]], axis=0)
    halo_cols = jnp.transpose(halo_cols, (2, 3, 0, 1)).reshape(faces, rows, 6 * levels)
    halo_cols = jnp.pad(halo_cols, ((0, 0), (0, 0), (0, LANES - 6 * levels)))
    damped = damp(fields, damp_four, damp_six, metric, halo_rows, halo_cols)
    return jnp.transpose(damped, (0, 2, 1, 3))


def solution(mesh):
    placed = (
        P("member", "ty", None, None),
        P("member"),
        P("member"),
        P(None, "ty", None, None),
        P(),
    )
    return jax.shard_map(
        per_device,
        mesh=mesh,
        in_specs=placed,
        out_specs=P("member", "ty", None, None),
        check_vma=False,
    )
```

time: 606 us -> 510 us (0.84)
  other arithmetic: 126 us -> 31.2 us
  local copies, waits for them, and re-layouts: 162 us -> 105 us
  Pallas kernels: 0 us -> 52.8 us
  starting transfers between devices: 15.1 us -> 38.7 us
  waiting for transfers between devices: 271 us -> 255 us
    add x4 -> x7, other arithmetic: 103 us -> 9.77 us  [the longest x6 9.77 us: weigh(): metric[0] * (west - cells) + metric[1] * (east - cells)]
    pallas_call x0 -> x1, Pallas kernels: none -> 52.8 us  [damp(): pl.pallas_call(damp_kernel, grid=(faces, levels // block), in_specs=[pl.B...]
    ppermute x6, starting transfers between devices: 15.1 us -> 38 us  [the longest x3 33.9 us: exchange(): below = lax.ppermute(north, 'ty', [(i, i + 1) for i in range(count - 1)])]
    broadcast_in_dim x11 -> x28, local copies, waits for them, and re-layouts: 29.2 us -> 8.69 us  [the longest x14 4.65 us: along_x(): west_halo[..., None]]
    reshape x8 -> x7, local copies, waits for them, and re-layouts: 27.1 us -> 7.51 us  [the longest x3 5.1 us: exchange(): edges = lax.psum(rim, 'ty').reshape(levels, faces * 4, width)]
    add x3 -> x4, local copies, waits for them, and re-layouts: 18.7 us -> 1.63 us  [the longest x2 1.46 us: weigh(): metric[0] * (west - cells) + metric[1] * (east - cells)]
    psum x3, waiting for transfers between devices: 271 us -> 255 us  [exchange(): edges = lax.psum(rim, 'ty').reshape(levels, faces * 4, width)]
    unnamed x19 -> x163, local copies, waits for them, and re-layouts: 28.6 us -> 14 us
  transfers between devices with their start and end apart: 9 -> 9, of which waited for: 3 -> 3; matrix products, arithmetic and copies ran while one was open for 14% -> 16% of each run, Pallas kernels for 0% -> 0%
where the time goes in v1:
time: 510 us; the launch traced here: 503 us
  waiting for transfers between devices  255 us (50%)
  local copies, waits for them, and re-layouts  105 us (21%)
  Pallas kernels  52.8 us (10%)
  starting transfers between devices  38.7 us (8%)
  other arithmetic  31.2 us (6%)
  between operations  15.1 us (3%)
  matrix products  5.82 us (1%)
    psum x3, waiting for transfers between devices, exchange(): edges = lax.psum(rim, 'ty').reshape(levels, faces * 4, width)  255 us
    pallas_call x1, Pallas kernels, damp(): pl.pallas_call(damp_kernel, grid=(faces, levels // block), in_specs=[pl.B...  52.8 us
    ppermute x3, starting transfers between devices, exchange(): below = lax.ppermute(north, 'ty', [(i, i + 1) for i in range(count - 1)])  33.9 us
    dynamic_update_slice x3, local copies, waits for them, and re-layouts, exchange(): placed = lax.dynamic_update_slice_in_dim(blank, sides, index * rows, 3)  15.1 us
    unnamed x163, local copies, waits for them, and re-layouts  14 us
  transfers between devices with their start and end apart: 9, of which 3 were waited for; matrix products, arithmetic and copies ran while one was open for 16% of the time, Pallas kernels for 0%

profile of v1, /device:TPU:0, one launch (start us, length us, event | category | flops | bytes accessed | tf_op | source)
XLA Modules:
  0.0 503.2 jit_solution(8139999430221239782)
XLA Ops:
  6.5 3.1 fusion.64
  10.5 3.1 collective-permute-start
  15.6 4.5 fusion.65
  20.1 2.5 copy.1747
  24.6 5.0 dynamic_update_slice.9
  31.6 1.7 copy.1642
  35.4 2.1 slice_bitcast_fusion.25
  52.6 6.8 %fusion.63 = (f32[16,6,2,767]{3,2,1,0:T(2,128)}, f32[16,6,2,767]{3,2,1,0:T(2,128)}, f32[16,6,2,767]{3,2,1,0:T(2,128)}, f32[16,6,2,767]{3,2,1,0:T(2,128)}) fusion(f32[16,6,48,768]{3,2,1,0:T(8,128)} %bitcast.191), kind=kLoop, calls=%fused_computation.187 | loop fusion | bytes 4712448 | tf_op jit(solution)/shard_map/slice | solution.py:63
  59.5 84.7 %all-reduce.6.cloned.1.call-done = f32[16,24,768]{2,1,0:T(8,128)} async-done(((f32[16,24,768]{2,1,0:T(8,128)}), f32[16,24,768]{2,1,0:T(8,128)}) %all-reduce.6.cloned.1.call-update) | async-done | bytes 1179664 | tf_op jit(solution)/shard_map/psum | solution.py:26
  144.1 1.9 convolution_bitcast_fusion.2
  147.2 1.8 rev.9
  162.0 5.0 dynamic_update_slice.10
  168.5 4.0 fusion.4
  173.5 4.1 fusion.2
  179.6 1.7 copy.1680
  184.8 15.8 %collective-permute-start.2 = (f32[16,6,768]{2,0,1:T(8,128)}, f32[16,6,768]{2,0,1:T(8,128)}, u32[]{:S(2)}, u32[]{:S(2)}) collective-permute-start(f32[16,6,768]{2,0,1:T(8,128)} %bitcast.174), channel_id=1, source_target_pairs={{0,1},{1,2},{2,3},{3,4},{4,5},{5,6},{6,7},{7,8},{8,9},{9,10},{10,1... | collective-permute-start | bytes 884744 | tf_op jit(solution)/shard_map/ppermute | solution.py:18
  202.2 1.9 fusion.72
  204.1 84.2 %all-reduce.8.cloned.1.call-done = f32[16,24,768]{2,1,0:T(8,128)} async-done(((f32[16,24,768]{2,1,0:T(8,128)}), f32[16,24,768]{2,1,0:T(8,128)}) %all-reduce.8.cloned.1.call-update) | async-done | bytes 1179664 | tf_op jit(solution)/shard_map/psum | solution.py:26
  288.3 1.9 convolution_bitcast_fusion.1
  291.4 3.3 rev.10
  294.7 2.2 broadcast_select_fusion.7
  303.8 5.0 dynamic_update_slice.11
  310.3 3.5 broadcast_select_fusion
  313.8 2.5 broadcast_select_fusion.3
  317.8 1.7 copy.1701
  322.4 15.0 %collective-permute-start.4 = (f32[16,6,768]{2,0,1:T(8,128)}, f32[16,6,768]{2,0,1:T(8,128)}, u32[]{:S(2)}, u32[]{:S(2)}) collective-permute-start(f32[16,6,768]{2,0,1:T(8,128)} %bitcast.172), channel_id=1, source_target_pairs={{0,1},{1,2},{2,3},{3,4},{4,5},{5,6},{6,7},{7,8},{8,9},{9,10},{10,1... | collective-permute-start | bytes 884744 | tf_op jit(solution)/shard_map/ppermute | solution.py:18
  340.2 86.0 %all-reduce.10.cloned.1.call-done = f32[16,24,768]{2,1,0:T(8,128)} async-done(((f32[16,24,768]{2,1,0:T(8,128)}), f32[16,24,768]{2,1,0:T(8,128)}) %all-reduce.10.cloned.1.call-update) | async-done | bytes 1179664 | tf_op jit(solution)/shard_map/psum | solution.py:26
  426.2 1.9 convolution_bitcast_fusion
  429.3 1.6 rev.11
  435.7 6.1 %stack.78 = f32[16,6,6,768]{3,2,1,0:T(8,128)S(1)} concatenate(f32[16,6,1,768]{3,2,1,0:T(1,128)S(1)} %copy-done.3, f32[16,6,1,768]{3,2,1,0:T(1,128)S(1)} %copy-done.1, f32[16,6,1,768]{3,2,1,0:T(1,128)} %get-tuple-element.91, f32[16,6,1,768]{3,2,1,0:T(1,128)} %get-tuple-element.92, f32[16,6,1,768]{3,2,1,0:T(1,128)S(1)} %copy.1713, f32[16,6,1,768]{3,2,1,0:T(1,128)S(1)} %copy.1714), dimensions={2} | concatenate | bytes 3538944 | tf_op jit(solution)/shard_map/stack | solution.py:207
  441.8 1.6 pad.8.hr_ref
  443.4 52.8 %damp.1 = f32[16,6,48,768]{3,2,1,0:T(8,128)} custom-call(f32[16]{0:T(128)} %four_ref.1, f32[16]{0:T(128)} %six_ref.1, f32[16,6,48,768]{3,2,1,0:T(8,128)} %bitcast.194, f32[4,6,48,768]{3,2,1,0:T(8,128)} %bitcast.204, f32[16,6,8,768]{3,2,1,0:T(8,128)} %pad.8.hr_ref, f32[6,48,128]{2,1,0:T(8,128)} %pad.9.hc_ref), custom_call_target="tpu_custom_call" | custom-call | flops 141557760 | bytes 35389440 | tf_op jit(solution)/shard_map/damp/pallas_call | solution.py:180
  (296 shorter events, 68.8 us)
Async XLA Ops:
  6.5 137.6 %all-reduce.6.cloned.1.call-start = ((), (), s32[]{:S(2)}) async-start(), calls=%async_computation | async-start | bytes 2359296 | tf_op jit(solution)/shard_map/psum | solution.py:26
  9.6 4.7 copy-start.4
  9.6 4.7 copy-start.6
  10.5 143.2 %collective-permute-start = (f32[16,6,768]{2,0,1:T(8,128)}, f32[16,6,768]{2,0,1:T(8,128)}, u32[]{:S(2)}, u32[]{:S(2)}) collective-permute-start(f32[16,6,768]{2,0,1:T(8,128)} %bitcast.176), channel_id=1, source_target_pairs={{0,1},{1,2},{2,3},{3,4},{4,5},{5,6},{6,7},{7,8},{8,9},{9,10},{10,1... | collective-permute-start | bytes 884744 | tf_op jit(solution)/shard_map/ppermute | solution.py:18
  14.3 137.1 %collective-permute-start.1 = (f32[16,6,768]{2,0,1:T(8,128)}, f32[16,6,768]{2,0,1:T(8,128)}, u32[]{:S(2)}, u32[]{:S(2)}) collective-permute-start(f32[16,6,768]{2,0,1:T(8,128)} %bitcast.175), channel_id=1, source_target_pairs={{1,0},{2,1},{3,2},{4,3},{5,4},{6,5},{7,6},{8,7},{9,8},{10,9},{11,1... | collective-permute-start | bytes 884744 | tf_op jit(solution)/shard_map/ppermute | solution.py:19
  22.7 29.2 %copy-start.12 = (f32[16,6,48,3]{2,3,1,0:T(4,128)}, f32[16,6,48,3]{2,3,1,0:T(4,128)S(1)}, u32[]{:S(2)}) copy-start(f32[16,6,48,3]{2,3,1,0:T(4,128)S(1)} %copy.1747) | copy-start | bytes 165892
  23.6 17.4 %copy-start.14 = (f32[16,6,48,3]{2,3,1,0:T(4,128)}, f32[16,6,48,3]{2,3,1,0:T(4,128)S(1)}, u32[]{:S(2)}) copy-start(f32[16,6,48,3]{2,3,1,0:T(4,128)S(1)} %copy.1748) | copy-start | bytes 165892
  33.3 255.0 %all-reduce.8.cloned.1.call-start = ((), (), s32[]{:S(2)}) async-start(), calls=%async_computation.1 | async-start | bytes 2359296 | tf_op jit(solution)/shard_map/psum | solution.py:26
  42.6 101.6 %copy-start.71 = (s32[24]{0:T(128)}, s32[24]{0:T(128)S(1)}, u32[]{:S(2)}) copy-start(s32[24]{0:T(128)S(1)} %add.107) | copy-start | bytes 292
  153.7 3.8 copy-start.13
  153.7 3.8 copy-start.26
  153.7 3.8 copy-start.36
  155.0 4.6 copy-start.18
  156.0 5.7 %copy-start.23 = (f32[16,6,1,48]{3,2,1,0:T(1,128)}, f32[16,6,1,48]{3,2,1,0:T(1,128)S(1)}, u32[]{:S(2)}) copy-start(f32[16,6,1,48]{3,2,1,0:T(1,128)S(1)} %constant_dynamic-slice_fusion.4) | copy-start | bytes 55300
  157.9 3.8 copy-start.16
  167.9 4.9 copy-start
  168.2 4.2 copy-start.2
  168.4 4.5 copy-start.5
  168.4 4.5 copy-start.9
  168.4 4.5 copy-start.44
  168.4 4.5 copy-start.45
  168.4 4.5 copy-start.46
  168.5 4.5 copy-start.47
  181.3 244.9 %all-reduce.10.cloned.1.call-start = ((), (), s32[]{:S(2)}) async-start(), calls=%async_computation.2 | async-start | bytes 2359296 | tf_op jit(solution)/shard_map/psum | solution.py:26
  182.7 115.1 %collective-permute-start.3 = (f32[16,6,768]{2,0,1:T(8,128)}, f32[16,6,768]{2,0,1:T(8,128)}, u32[]{:S(2)}, u32[]{:S(2)}) collective-permute-start(f32[16,6,768]{2,0,1:T(8,128)} %bitcast.173), channel_id=1, source_target_pairs={{1,0},{2,1},{3,2},{4,3},{5,4},{6,5},{7,6},{8,7},{9,8},{10,9},{11,1... | collective-permute-start | bytes 884744 | tf_op jit(solution)/shard_map/ppermute | solution.py:19
  184.8 103.5 %copy-start.72 = (s32[24]{0:T(128)S(1)}, s32[24]{0:T(128)}, u32[]{:S(2)}) copy-start(s32[24]{0:T(128)} %copy-done.71) | copy-start | bytes 292
  184.8 114.4 %collective-permute-start.2 = (f32[16,6,768]{2,0,1:T(8,128)}, f32[16,6,768]{2,0,1:T(8,128)}, u32[]{:S(2)}, u32[]{:S(2)}) collective-permute-start(f32[16,6,768]{2,0,1:T(8,128)} %bitcast.174), channel_id=1, source_target_pairs={{0,1},{1,2},{2,3},{3,4},{4,5},{5,6},{6,7},{7,8},{8,9},{9,10},{10,1... | collective-permute-start | bytes 884744 | tf_op jit(solution)/shard_map/ppermute | solution.py:18
  303.0 7.2 %copy-start.22 = (f32[16,6,1,767]{3,2,1,0:T(1,128)S(1)}, f32[16,6,1,767]{3,2,1,0:T(1,128)}, u32[]{:S(2)}) copy-start(f32[16,6,1,767]{3,2,1,0:T(1,128)} %get-tuple-element.73) | copy-start | bytes 883588
  319.5 19.5 %copy-start.30 = (f32[16,6,1,48]{3,2,1,0:T(1,128)S(1)}, f32[16,6,1,48]{3,2,1,0:T(1,128)}, u32[]{:S(2)}) copy-start(f32[16,6,1,48]{3,2,1,0:T(1,128)} %copy-done.29) | copy-start | bytes 55300
  319.5 20.1 %copy-start.32 = (f32[16,6,1,48]{3,2,1,0:T(1,128)S(1)}, f32[16,6,1,48]{3,2,1,0:T(1,128)}, u32[]{:S(2)}) copy-start(f32[16,6,1,48]{3,2,1,0:T(1,128)} %copy-done.31) | copy-start | bytes 55300
  322.4 110.4 %collective-permute-start.4 = (f32[16,6,768]{2,0,1:T(8,128)}, f32[16,6,768]{2,0,1:T(8,128)}, u32[]{:S(2)}, u32[]{:S(2)}) collective-permute-start(f32[16,6,768]{2,0,1:T(8,128)} %bitcast.172), channel_id=1, source_target_pairs={{0,1},{1,2},{2,3},{3,4},{4,5},{5,6},{6,7},{7,8},{8,9},{9,10},{10,1... | collective-permute-start | bytes 884744 | tf_op jit(solution)/shard_map/ppermute | solution.py:18
  337.4 95.8 %collective-permute-start.5 = (f32[16,6,768]{2,0,1:T(8,128)}, f32[16,6,768]{2,0,1:T(8,128)}, u32[]{:S(2)}, u32[]{:S(2)}) collective-permute-start(f32[16,6,768]{2,0,1:T(8,128)} %bitcast.171), channel_id=1, source_target_pairs={{1,0},{2,1},{3,2},{4,3},{5,4},{6,5},{7,6},{8,7},{9,8},{10,9},{11,1... | collective-permute-start | bytes 884744 | tf_op jit(solution)/shard_map/ppermute | solution.py:19
  (51 other events, 125.5 us)
Sparse Core Ops, SparseCore 0:
  33.4 110.6 all-reduce.5
  181.5 106.7 all-reduce.7
  319.6 106.5 all-reduce.9
